TPU v7x, 32 devices: a whole 2x2x4 slice. The times are simulated.
32 devices in a mesh: row: 8 (over z, core), col: 4 (over y, x).
Axes of the slice: x: 2, y: 2, z: 4, core: 2. Of those that a mesh axis runs over, the one named last changes fastest.
Arguments:
- matrix: bfloat16 [12288, 12288], P('row', 'col'), may hold values from -8 to 8, as said below
- panels: bfloat16 [2, 12288, 128], P(None, 'row'), may hold values from -1 to 1
Outputs:
- updated: bfloat16 [12288, 12288], P('row', 'col')
Inputs may be any that keep to these rules, and one draw needn't show every extreme that they name: matrix is exactly symmetric.
All inputs are finite; a program needn't handle non-finite values.
Results may differ from a plain program's by a relative error of at most 0.015.
Values may be sent and summed in bfloat16 or wider, within the bound.
No kernel may reach another device: no remote copies, remote signals or barrier semaphores. Data moves between devices by JAX's collectives and lax.ppermute only.
A program may use at most 128 MiB of HBM per device.

v0:
```python
import jax
import jax.numpy as jnp
from jax import lax
from jax.sharding import PartitionSpec as P

PANELS = 2


def spread(block, axis, source):
    block = jnp.where(lax.axis_index(axis) == source, block, jnp.zeros_like(block))
    return lax.psum(block, axis)


def per_device(matrix, panels):
    row_count = lax.axis_size("row")
    col_count = lax.axis_size("col")
    owner_ratio = row_count // col_count
    row_index = lax.axis_index("row")
    col_index = lax.axis_index("col")
    a_tile = matrix
    n_rows = a_tile.shape[0]
    n_cols = a_tile.shape[1]
    for panel in range(PANELS):
        v_rows = panels[panel]
        gathered = lax.all_gather(v_rows, "row", axis=0, tiled=True)
        v_cols = lax.dynamic_slice_in_dim(gathered, col_index * n_cols, n_cols, 0)
        tile_now = a_tile
        av_fine = lax.psum_scatter(
            lax.dot_general(
                tile_now, v_rows, (((0,), (0,)), ((), ())), preferred_element_type=jnp.float32
            ),
            "row",
            scatter_dimension=0,
            tiled=True,
        )
        av_cols = lax.all_gather(av_fine, "row", axis=0, tiled=True)
        own_rows = lax.dynamic_slice_in_dim(av_cols, row_index % owner_ratio * n_rows, n_rows, 0)
        av_rows = spread(own_rows, "col", row_index // owner_ratio)
        local_sum = jnp.dot(v_rows.astype(jnp.float32).T, av_rows, precision=lax.Precision.HIGHEST)
        curvature = lax.psum(local_sum.astype(jnp.bfloat16), "row").astype(jnp.float32)
        w_cols = (
            av_cols
            - 0.5 * jnp.dot(v_cols.astype(jnp.float32), curvature, precision=lax.Precision.HIGHEST)
        ).astype(jnp.bfloat16)
        w_rows = (
            av_rows
            - 0.5 * jnp.dot(v_rows.astype(jnp.float32), curvature, precision=lax.Precision.HIGHEST)
        ).astype(jnp.bfloat16)
        update = lax.dot_general(
            v_rows, w_cols, (((1,), (1,)), ((), ())), preferred_element_type=jnp.float32
        )
        update = update + lax.dot_general(
            w_rows, v_cols, (((1,), (1,)), ((), ())), preferred_element_type=jnp.float32
        )
        a_tile = (a_tile.astype(jnp.float32) - update).astype(jnp.bfloat16)
    return a_tile


def solution(mesh):
    in_specs = (P("row", "col"), P(None, "row", None))
    out_specs = P("row", "col")
    return jax.shard_map(
        per_device, mesh=mesh, in_specs=in_specs, out_specs=out_specs, check_vma=False
    )
```

profile of v0, /device:TPU:0, one launch (start us, length us, event | category | flops | bytes accessed | tf_op | source)
XLA Modules:
  0.0 393.4 jit_solution(9624634092060317979)
XLA Ops:
  6.5 7.5 %fusion.34 = f32[3072,128]{1,0:T(8,128)} fusion(bf16[1536,3072]{1,0:T(8,128)(2,1)} %param.2, bf16[2,1536,128]{2,1,0:T(8,128)(2,1)} %param.3), kind=kOutput, calls=%fused_computation.44 | convolution fusion | flops 1207959552 | bytes 11403264 | tf_op jit(solution)/shard_map/dot_general | solution.py:29
  14.2 37.0 %reduce-scatter.3.cloned.1.call-done = f32[384,128]{1,0:T(8,128)} async-done(((f32[3072,128]{1,0:T(8,128)}), f32[384,128]{1,0:T(8,128)}) %reduce-scatter.3.cloned.1.call-update) | async-done | bytes 196624 | tf_op jit(solution)/shard_map/reduce_scatter | solution.py:28
  51.2 25.2 %all-gather.7.cloned.1.call-done = f32[3072,128]{1,0:T(8,128)} async-done(((f32[384,128]{1,0:T(8,128)}), f32[3072,128]{1,0:T(8,128)}) %all-gather.7.cloned.1.call-update) | async-done | bytes 1572880 | tf_op jit(solution)/shard_map/all_gather | solution.py:36
  76.4 2.1 dynamic-slice_select_fusion.1
  79.6 12.8 %copy.3 = bf16[1536,3072]{0,1:T(8,128)(2,1)} copy(bf16[1536,3072]{1,0:T(8,128)(2,1)} %param.2) | data formatting | bytes 18874368 | tf_op args[0]
  92.3 34.9 %all-reduce.3.cloned.1.call-done = f32[1536,128]{1,0:T(8,128)} async-done(((f32[1536,128]{1,0:T(8,128)}), f32[1536,128]{1,0:T(8,128)}) %all-reduce.3.cloned.1.call-update) | async-done | bytes 786448 | tf_op jit(solution)/shard_map/psum | solution.py:11
  127.3 1.9 fusion.14
  129.2 29.9 %psum.29 = bf16[128,128]{0,1:T(8,128)(2,1)S(1)} all-reduce(bf16[128,128]{0,1:T(8,128)(2,1)S(1)} %fusion.14), channel_id=1, replica_groups=mesh['row'=8,'col'=4] {'row'}, use_global_device_ids=true, to_apply=%region_2.3 | all-reduce | flops 16384 | bytes 65536 | tf_op jit(solution)/shard_map/psum | solution.py:40
  159.1 8.3 %all-gather.11.cloned.1.call-done = bf16[1,12288,128]{2,1,0:T(8,128)(2,1)} async-done(((bf16[1,1536,128]{2,1,0:T(8,128)(2,1)}), bf16[1,12288,128]{2,1,0:T(8,128)(2,1)}) %all-gather.11.cloned.1.call-update) | async-done | bytes 3145744 | tf_op jit(solution)/shard_map/all_gather | solution.py:25
  167.4 1.5 fusion.6
  168.9 8.0 %fusion.30 = f32[3072,1536]{1,0:T(8,128)} fusion(bf16[3072,128]{1,0:T(8,128)(2,1)S(1)} %fusion.6, bf16[2,1536,128]{2,1,0:T(8,128)(2,1)S(1)} %copy-done), kind=kOutput, calls=%fused_computation.40 | convolution fusion | flops 1207959552 | bytes 20054016 | tf_op jit(solution)/shard_map/dot_general | solution.py:49
  177.2 14.6 %fusion.3 = bf16[1536,3072]{0,1:T(8,128)(2,1)} fusion(f32[3072,1536]{1,0:T(8,128)} %fusion.30, bf16[1536,3072]{0,1:T(8,128)(2,1)} %copy.3, bf16[1536,128]{1,0:T(8,128)(2,1)S(1)} %fusion.13, bf16[1,12288,128]{2,1,0:T(8,128)(2,1)} %all-gather.11.cloned.1.call-done, s32[]{:T(128)S(6)} %select_n.34), kind=kOutput, calls=%fused_computation.5 | convolution fusion | flops 1226833920 | bytes 38928388 | tf_op jit(solution)/shard_map/dot_general | solution.py:52
  191.8 7.5 %fusion.28 = f32[3072,128]{1,0:T(8,128)} fusion(bf16[1536,3072]{0,1:T(8,128)(2,1)} %fusion.3, bf16[2,1536,128]{2,1,0:T(8,128)(2,1)S(1)} %copy-done), kind=kOutput, calls=%fused_computation.38 | convolution fusion | flops 1207959552 | bytes 11403264 | tf_op jit(solution)/shard_map/dot_general | solution.py:29
  199.3 33.1 %reduce-scatter.5.cloned.1.call-done = f32[384,128]{1,0:T(8,128)} async-done(((f32[3072,128]{1,0:T(8,128)}), f32[384,128]{1,0:T(8,128)}) %reduce-scatter.5.cloned.1.call-update) | async-done | bytes 196624 | tf_op jit(solution)/shard_map/reduce_scatter | solution.py:28
  232.5 25.2 %all-gather.9.cloned.1.call-done = f32[3072,128]{1,0:T(8,128)} async-done(((f32[384,128]{1,0:T(8,128)}), f32[3072,128]{1,0:T(8,128)}) %all-gather.9.cloned.1.call-update) | async-done | bytes 1572880 | tf_op jit(solution)/shard_map/all_gather | solution.py:36
  257.7 2.1 dynamic-slice_select_fusion
  260.6 48.0 %all-reduce.5.cloned.1.call-done = f32[1536,128]{1,0:T(8,128)} async-done(((f32[1536,128]{1,0:T(8,128)}), f32[1536,128]{1,0:T(8,128)}) %all-reduce.5.cloned.1.call-update) | async-done | bytes 786448 | tf_op jit(solution)/shard_map/psum | solution.py:11
  308.6 1.9 fusion.15
  310.5 30.2 %psum.31 = bf16[128,128]{0,1:T(8,128)(2,1)S(1)} all-reduce(bf16[128,128]{0,1:T(8,128)(2,1)S(1)} %fusion.15), channel_id=1, replica_groups=mesh['row'=8,'col'=4] {'row'}, use_global_device_ids=true, to_apply=%region_5.6 | all-reduce | flops 16384 | bytes 65536 | tf_op jit(solution)/shard_map/psum | solution.py:40
  340.7 8.1 %all-gather.13.cloned.1.call-done = bf16[1,12288,128]{2,1,0:T(8,128)(2,1)} async-done(((bf16[1,1536,128]{2,1,0:T(8,128)(2,1)}), bf16[1,12288,128]{2,1,0:T(8,128)(2,1)}) %all-gather.13.cloned.1.call-update) | async-done | bytes 3145744 | tf_op jit(solution)/shard_map/all_gather | solution.py:25
  348.8 2.0 fusion.7
  350.9 8.0 %fusion.24 = f32[3072,1536]{1,0:T(8,128)} fusion(bf16[3072,128]{1,0:T(8,128)(2,1)S(1)} %fusion.7, bf16[2,1536,128]{2,1,0:T(8,128)(2,1)S(1)} %copy-done), kind=kOutput, calls=%fused_computation.34 | convolution fusion | flops 1207959552 | bytes 20054016 | tf_op jit(solution)/shard_map/dot_general | solution.py:49
  359.1 14.8 %fusion.1 = bf16[1536,3072]{0,1:T(8,128)(2,1)} fusion(f32[3072,1536]{1,0:T(8,128)} %fusion.24, bf16[1536,3072]{0,1:T(8,128)(2,1)} %fusion.3, bf16[1536,128]{1,0:T(8,128)(2,1)S(1)} %fusion.12, bf16[1,12288,128]{2,1,0:T(8,128)(2,1)} %all-gather.13.cloned.1.call-done, s32[]{:T(128)S(6)} %select_n.34), kind=kOutput, calls=%fused_computation.2 | convolution fusion | flops 1226833920 | bytes 38928388 | tf_op jit(solution)/shard_map/dot_general | solution.py:52
  374.0 12.6 %copy.6 = bf16[1536,3072]{1,0:T(8,128)(2,1)} copy(bf16[1536,3072]{0,1:T(8,128)(2,1)} %fusion.1) | data formatting | bytes 18874368 | tf_op jit(solution)/shard_map/convert_element_type | solution.py:55
  (27 shorter events, 2.6 us)
Async XLA Ops:
  6.5 72.0 %copy-start = (bf16[2,1536,128]{2,1,0:T(8,128)(2,1)S(1)}, bf16[2,1536,128]{2,1,0:T(8,128)(2,1)}, u32[]{:S(2)}) copy-start(bf16[2,1536,128]{2,1,0:T(8,128)(2,1)} %param.3) | copy-start | bytes 2359300
  6.5 44.6 %reduce-scatter.3.cloned.1.call-start = ((), (), s32[]{:S(2)}) async-start(), calls=%async_computation.2 | async-start | bytes 1769472 | tf_op jit(solution)/shard_map/reduce_scatter | solution.py:28
  14.1 62.3 %all-gather.7.cloned.1.call-start = ((), (), s32[]{:S(2)}) async-start(), calls=%async_computation.3 | async-start | bytes 1769472 | tf_op jit(solution)/shard_map/all_gather | solution.py:36
  51.2 76.1 %all-reduce.3.cloned.1.call-start = ((), (), s32[]{:S(2)}) async-start(), calls=%async_computation.4 | async-start | bytes 1572864 | tf_op jit(solution)/shard_map/psum | solution.py:11
  78.5 88.9 %all-gather.11.cloned.1.call-start = ((), (), s32[]{:S(2)}) async-start(), calls=%async_computation.8 | async-start | bytes 3538944 | tf_op jit(solution)/shard_map/all_gather | solution.py:25
  79.5 152.9 %reduce-scatter.5.cloned.1.call-start = ((), (), s32[]{:S(2)}) async-start(), calls=%async_computation.5 | async-start | bytes 1769472 | tf_op jit(solution)/shard_map/reduce_scatter | solution.py:28
  79.5 87.9 %copy-start.1 = (f32[3072,128]{1,0:T(8,128)S(1)}, f32[3072,128]{1,0:T(8,128)}, u32[]{:S(2)}) copy-start(f32[3072,128]{1,0:T(8,128)} %all-gather.7.cloned.1.call-done) | copy-start | bytes 4718596
  168.9 8.0 %copy-start.2 = (f32[1536,128]{1,0:T(8,128)S(1)}, f32[1536,128]{1,0:T(8,128)}, u32[]{:S(2)}) copy-start(f32[1536,128]{1,0:T(8,128)} %all-reduce.3.cloned.1.call-done) | copy-start | bytes 2359300
  199.2 58.5 %all-gather.9.cloned.1.call-start = ((), (), s32[]{:S(2)}) async-start(), calls=%async_computation.6 | async-start | bytes 1769472 | tf_op jit(solution)/shard_map/all_gather | solution.py:36
  232.5 76.1 %all-reduce.5.cloned.1.call-start = ((), (), s32[]{:S(2)}) async-start(), calls=%async_computation.7 | async-start | bytes 1572864 | tf_op jit(solution)/shard_map/psum | solution.py:11
  259.8 89.0 %all-gather.13.cloned.1.call-start = ((), (), s32[]{:S(2)}) async-start(), calls=%async_computation.9 | async-start | bytes 3538944 | tf_op jit(solution)/shard_map/all_gather | solution.py:25
  350.9 8.0 %copy-start.3 = (f32[1536,128]{1,0:T(8,128)S(1)}, f32[1536,128]{1,0:T(8,128)}, u32[]{:S(2)}) copy-start(f32[1536,128]{1,0:T(8,128)} %all-reduce.5.cloned.1.call-done) | copy-start | bytes 2359300
Sparse Core Ops, SparseCore 0:
  14.2 36.8 reduce-scatter.2
  52.8 23.5 all-gather.6
  79.5 47.7 all-reduce.2
  128.8 38.5 all-gather.10
  199.4 33.0 reduce-scatter.4
  233.9 23.7 all-gather.8
  260.7 47.7 all-reduce.4
  310.2 38.6 all-gather.12
where the time goes:
time: 394 us; the launch traced here: 393 us
  waiting for transfers between devices  221 us (56%)
  matrix products  68.3 us (17%)
  blocking collectives  60.1 us (15%)
  local copies, waits for them, and re-layouts  26.3 us (7%)
  between operations  13.6 us (3%)
  other arithmetic  4.14 us (1%)
    psum x2, waiting for transfers between devices, spread(): return lax.psum(block, axis)  82.9 us
    reduce_scatter x2, waiting for transfers between devices, per_device(): lax.psum_scatter(lax.dot_general(tile_now, v_rows, (((0,), (0,)), ((), ()...  70.1 us
    psum x2, blocking collectives, per_device(): lax.psum(local_sum.astype(jnp.bfloat16), 'row').astype(jnp.float32)  60.1 us
    all_gather x2, waiting for transfers between devices, per_device(): av_cols = lax.all_gather(av_fine, 'row', axis=0, tiled=True)  50.3 us
    dot_general x2, matrix products, per_device(): lax.dot_general(w_rows, v_cols, (((1,), (1,)), ((), ())), preferred_eleme...  29.4 us
    all_gather x2, waiting for transfers between devices, per_device(): gathered = lax.all_gather(v_rows, 'row', axis=0, tiled=True)  16.4 us
    dot_general x2, matrix products, per_device(): lax.dot_general(v_rows, w_cols, (((1,), (1,)), ((), ())), preferred_eleme...  16 us
    dot_general x2, matrix products, per_device(): lax.dot_general(tile_now, v_rows, (((0,), (0,)), ((), ())), preferred_ele...  15 us
  transfers between devices with their start and end apart: 8, of which 8 were waited for; matrix products, arithmetic and copies ran while one was open for 4% of the time, Pallas kernels for 0%

commit v1 on v0

--- a/solution.py
+++ b/solution.py
@@ -6,9 +6,15 @@
 PANELS = 2
 
 
+def summed_here(array, mesh_axis):
+    parts = lax.all_gather(array, mesh_axis, axis=0, tiled=False)
+    total = parts.sum(axis=0)
+    return total
+
+
 def spread(block, axis, source):
     block = jnp.where(lax.axis_index(axis) == source, block, jnp.zeros_like(block))
-    return lax.psum(block, axis)
+    return summed_here(block, axis)
 
 
 def per_device(matrix, panels):

time: 394 us -> 382 us (0.970)
  waiting for transfers between devices: 221 us -> 204 us
  other arithmetic: 4.14 us -> 8.69 us
    psum x2 -> x0, waiting for transfers between devices: 82.9 us -> none  [spread(): return lax.psum(block, axis)]
    all_gather x0 -> x2, waiting for transfers between devices: none -> 71.8 us  [summed_here(): parts = lax.all_gather(array, mesh_axis, axis=0, tiled=False)]
    all_gather x2, waiting for transfers between devices: 16.4 us -> 10.9 us  [per_device(): gathered = lax.all_gather(v_rows, 'row', axis=0, tiled=True)]
    reduce_sum x0 -> x2, other arithmetic: none -> 4.5 us  [summed_here(): total = parts.sum(axis=0)]
    unnamed x9 -> x7, local copies, waits for them, and re-layouts: 12.8 us -> 12.6 us
  transfers between devices with their start and end apart: 8 -> 8, of which waited for: 8 -> 8; matrix products, arithmetic and copies ran while one was open for 4% -> 6% of each run, Pallas kernels for 0% -> 0%
where the time goes in v1:
time: 382 us; the launch traced here: 381 us
  waiting for transfers between devices  204 us (53%)
  matrix products  66.6 us (17%)
  blocking collectives  61.4 us (16%)
  local copies, waits for them, and re-layouts  26.2 us (7%)
  between operations  13.6 us (4%)
  other arithmetic  8.69 us (2%)
    all_gather x2, waiting for transfers between devices, summed_here(): parts = lax.all_gather(array, mesh_axis, axis=0, tiled=False)  71.8 us
    reduce_scatter x2, waiting for transfers between devices, per_device(): lax.psum_scatter(lax.dot_general(tile_now, v_rows, (((0,), (0,)), ((), ()...  70.2 us
    psum x2, blocking collectives, per_device(): lax.psum(local_sum.astype(jnp.bfloat16), 'row').astype(jnp.float32)  61.4 us
    all_gather x2, waiting for transfers between devices, per_device(): av_cols = lax.all_gather(av_fine, 'row', axis=0, tiled=True)  50.2 us
    dot_general x2, matrix products, per_device(): lax.dot_general(w_rows, v_cols, (((1,), (1,)), ((), ())), preferred_eleme...  29.3 us
    dot_general x2, matrix products, per_device(): lax.dot_general(v_rows, w_cols, (((1,), (1,)), ((), ())), preferred_eleme...  15.8 us
    dot_general x2, matrix products, per_device(): lax.dot_general(tile_now, v_rows, (((0,), (0,)), ((), ())), preferred_ele...  14.9 us
    convert_element_type x1, local copies, waits for them, and re-layouts, per_device(): a_tile = (a_tile.astype(jnp.float32) - update).astype(jnp.bfloat16)  12.6 us
  transfers between devices with their start and end apart: 8, of which 8 were waited for; matrix products, arithmetic and copies ran while one was open for 6% of the time, Pallas kernels for 0%

profile of v1, /device:TPU:0, one launch (start us, length us, event | category | flops | bytes accessed | tf_op | source)
XLA Modules:
  0.0 380.6 jit_solution(10509218404328819824)
XLA Ops:
  6.5 7.5 %fusion.34 = f32[3072,128]{1,0:T(8,128)} fusion(bf16[1536,3072]{1,0:T(8,128)(2,1)} %param.2, bf16[2,1536,128]{2,1,0:T(8,128)(2,1)} %param.3), kind=kOutput, calls=%fused_computation.44 | convolution fusion | flops 1207959552 | bytes 11403264 | tf_op jit(solution)/shard_map/dot_general | solution.py:35
  14.1 37.0 %reduce-scatter.3.cloned.1.call-done = f32[384,128]{1,0:T(8,128)} async-done(((f32[3072,128]{1,0:T(8,128)}), f32[384,128]{1,0:T(8,128)}) %reduce-scatter.3.cloned.1.call-update) | async-done | bytes 196624 | tf_op jit(solution)/shard_map/reduce_scatter | solution.py:34
  51.2 25.2 %all-gather.11.cloned.1.call-done = f32[3072,128]{1,0:T(8,128)} async-done(((f32[384,128]{1,0:T(8,128)}), f32[3072,128]{1,0:T(8,128)}) %all-gather.11.cloned.1.call-update) | async-done | bytes 1572880 | tf_op jit(solution)/shard_map/all_gather | solution.py:42
  76.3 2.1 dynamic-slice_select_fusion.1
  79.6 12.6 %copy.3 = bf16[1536,3072]{0,1:T(8,128)(2,1)} copy(bf16[1536,3072]{1,0:T(8,128)(2,1)} %param.2) | data formatting | bytes 18874368 | tf_op args[0]
  92.2 29.4 %all-gather.17.cloned.1.call-done = f32[6144,128]{1,0:T(8,128)} async-done(((f32[1536,128]{1,0:T(8,128)}), f32[6144,128]{1,0:T(8,128)}) %all-gather.17.cloned.1.call-update) | async-done | bytes 3145744 | tf_op jit(solution)/shard_map/all_gather | solution.py:10
  121.6 2.2 reduce_sum.18
  124.6 30.7 %psum.14 = bf16[128,128]{0,1:T(8,128)(2,1)} all-reduce(bf16[128,128]{0,1:T(8,128)(2,1)S(1)} %fusion.14), channel_id=1, replica_groups=mesh['row'=8,'col'=4] {'row'}, use_global_device_ids=true, to_apply=%region_2.3 | all-reduce | flops 16384 | bytes 65536 | tf_op jit(solution)/shard_map/psum | solution.py:46
  156.4 5.4 %all-gather.15.cloned.1.call-done = bf16[1,12288,128]{2,1,0:T(8,128)(2,1)} async-done(((bf16[1,1536,128]{2,1,0:T(8,128)(2,1)}), bf16[1,12288,128]{2,1,0:T(8,128)(2,1)}) %all-gather.15.cloned.1.call-update) | async-done | bytes 3145744 | tf_op jit(solution)/shard_map/all_gather | solution.py:31
  161.8 1.5 fusion.6
  163.3 7.9 %fusion.30 = f32[3072,1536]{1,0:T(8,128)} fusion(bf16[3072,128]{1,0:T(8,128)(2,1)S(1)} %fusion.6, bf16[2,1536,128]{2,1,0:T(8,128)(2,1)S(1)} %copy-done), kind=kOutput, calls=%fused_computation.40 | convolution fusion | flops 1207959552 | bytes 20054016 | tf_op jit(solution)/shard_map/dot_general | solution.py:55
  171.2 14.6 %fusion.3 = bf16[1536,3072]{0,1:T(8,128)(2,1)} fusion(f32[3072,1536]{1,0:T(8,128)} %fusion.30, bf16[1536,3072]{0,1:T(8,128)(2,1)} %copy.3, bf16[1536,128]{1,0:T(8,128)(2,1)S(1)} %fusion.13, bf16[1,12288,128]{2,1,0:T(8,128)(2,1)} %all-gather.15.cloned.1.call-done, s32[]{:T(128)S(6)} %select_n.34), kind=kOutput, calls=%fused_computation.5 | convolution fusion | flops 1226833920 | bytes 38928388 | tf_op jit(solution)/shard_map/dot_general | solution.py:58
  185.7 7.4 %fusion.28 = f32[3072,128]{1,0:T(8,128)} fusion(bf16[1536,3072]{0,1:T(8,128)(2,1)} %fusion.3, bf16[2,1536,128]{2,1,0:T(8,128)(2,1)S(1)} %copy-done), kind=kOutput, calls=%fused_computation.38 | convolution fusion | flops 1207959552 | bytes 11403264 | tf_op jit(solution)/shard_map/dot_general | solution.py:35
  193.3 33.2 %reduce-scatter.5.cloned.1.call-done = f32[384,128]{1,0:T(8,128)} async-done(((f32[3072,128]{1,0:T(8,128)}), f32[384,128]{1,0:T(8,128)}) %reduce-scatter.5.cloned.1.call-update) | async-done | bytes 196624 | tf_op jit(solution)/shard_map/reduce_scatter | solution.py:34
  226.5 25.0 %all-gather.13.cloned.1.call-done = f32[3072,128]{1,0:T(8,128)} async-done(((f32[384,128]{1,0:T(8,128)}), f32[3072,128]{1,0:T(8,128)}) %all-gather.13.cloned.1.call-update) | async-done | bytes 1572880 | tf_op jit(solution)/shard_map/all_gather | solution.py:42
  251.5 2.1 dynamic-slice_select_fusion
  254.4 42.4 %all-gather.21.cloned.1.call-done = f32[6144,128]{1,0:T(8,128)} async-done(((f32[1536,128]{1,0:T(8,128)}), f32[6144,128]{1,0:T(8,128)}) %all-gather.21.cloned.1.call-update) | async-done | bytes 3145744 | tf_op jit(solution)/shard_map/all_gather | solution.py:10
  296.8 2.2 reduce_sum.19
  299.8 30.7 %psum.15 = bf16[128,128]{0,1:T(8,128)(2,1)} all-reduce(bf16[128,128]{0,1:T(8,128)(2,1)S(1)} %fusion.15), channel_id=1, replica_groups=mesh['row'=8,'col'=4] {'row'}, use_global_device_ids=true, to_apply=%region_5.6 | all-reduce | flops 16384 | bytes 65536 | tf_op jit(solution)/shard_map/psum | solution.py:46
  331.6 5.5 %all-gather.19.cloned.1.call-done = bf16[1,12288,128]{2,1,0:T(8,128)(2,1)} async-done(((bf16[1,1536,128]{2,1,0:T(8,128)(2,1)}), bf16[1,12288,128]{2,1,0:T(8,128)(2,1)}) %all-gather.19.cloned.1.call-update) | async-done | bytes 3145744 | tf_op jit(solution)/shard_map/all_gather | solution.py:31
  337.1 1.5 fusion.7
  338.6 7.9 %fusion.24 = f32[3072,1536]{1,0:T(8,128)} fusion(bf16[3072,128]{1,0:T(8,128)(2,1)S(1)} %fusion.7, bf16[2,1536,128]{2,1,0:T(8,128)(2,1)S(1)} %copy-done), kind=kOutput, calls=%fused_computation.34 | convolution fusion | flops 1207959552 | bytes 20054016 | tf_op jit(solution)/shard_map/dot_general | solution.py:55
  346.5 14.7 %fusion.1 = bf16[1536,3072]{0,1:T(8,128)(2,1)} fusion(f32[3072,1536]{1,0:T(8,128)} %fusion.24, bf16[1536,3072]{0,1:T(8,128)(2,1)} %fusion.3, bf16[1536,128]{1,0:T(8,128)(2,1)S(1)} %fusion.12, bf16[1,12288,128]{2,1,0:T(8,128)(2,1)} %all-gather.19.cloned.1.call-done, s32[]{:T(128)S(6)} %select_n.34), kind=kOutput, calls=%fused_computation.2 | convolution fusion | flops 1226833920 | bytes 38928388 | tf_op jit(solution)/shard_map/dot_general | solution.py:58
  361.2 12.6 %copy.6 = bf16[1536,3072]{1,0:T(8,128)(2,1)} copy(bf16[1536,3072]{0,1:T(8,128)(2,1)} %fusion.1) | data formatting | bytes 18874368 | tf_op jit(solution)/shard_map/convert_element_type | solution.py:61
  (27 shorter events, 5.7 us)
Async XLA Ops:
  6.5 44.5 %reduce-scatter.3.cloned.1.call-start = ((), (), s32[]{:S(2)}) async-start(), calls=%async_computation.2 | async-start | bytes 1769472 | tf_op jit(solution)/shard_map/reduce_scatter | solution.py:34
  14.0 64.5 %copy-start = (bf16[2,1536,128]{2,1,0:T(8,128)(2,1)S(1)}, bf16[2,1536,128]{2,1,0:T(8,128)(2,1)}, u32[]{:S(2)}) copy-start(bf16[2,1536,128]{2,1,0:T(8,128)(2,1)} %param.3) | copy-start | bytes 2359300
  14.0 62.3 %all-gather.11.cloned.1.call-start = ((), (), s32[]{:S(2)}) async-start(), calls=%async_computation.3 | async-start | bytes 1769472 | tf_op jit(solution)/shard_map/all_gather | solution.py:42
  51.1 70.5 %all-gather.17.cloned.1.call-start = ((), (), s32[]{:S(2)}) async-start(), calls=%async_computation.7 | async-start | bytes 3932160 | tf_op jit(solution)/shard_map/all_gather | solution.py:10
  78.4 83.3 %all-gather.15.cloned.1.call-start = ((), (), s32[]{:S(2)}) async-start(), calls=%async_computation.6 | async-start | bytes 3538944 | tf_op jit(solution)/shard_map/all_gather | solution.py:31
  79.5 146.9 %reduce-scatter.5.cloned.1.call-start = ((), (), s32[]{:S(2)}) async-start(), calls=%async_computation.4 | async-start | bytes 1769472 | tf_op jit(solution)/shard_map/reduce_scatter | solution.py:34
  121.6 40.2 %copy-start.1 = (f32[3072,128]{1,0:T(8,128)S(1)}, f32[3072,128]{1,0:T(8,128)}, u32[]{:S(2)}) copy-start(f32[3072,128]{1,0:T(8,128)} %all-gather.11.cloned.1.call-done) | copy-start | bytes 4718596
  193.2 58.3 %all-gather.13.cloned.1.call-start = ((), (), s32[]{:S(2)}) async-start(), calls=%async_computation.5 | async-start | bytes 1769472 | tf_op jit(solution)/shard_map/all_gather | solution.py:42
  226.5 70.3 %all-gather.21.cloned.1.call-start = ((), (), s32[]{:S(2)}) async-start(), calls=%async_computation.9 | async-start | bytes 3932160 | tf_op jit(solution)/shard_map/all_gather | solution.py:10
  253.6 83.4 %all-gather.19.cloned.1.call-start = ((), (), s32[]{:S(2)}) async-start(), calls=%async_computation.8 | async-start | bytes 3538944 | tf_op jit(solution)/shard_map/all_gather | solution.py:31
  296.8 40.3 %copy-start.2 = (f32[3072,128]{1,0:T(8,128)S(1)}, f32[3072,128]{1,0:T(8,128)}, u32[]{:S(2)}) copy-start(f32[3072,128]{1,0:T(8,128)} %all-gather.13.cloned.1.call-done) | copy-start | bytes 4718596
Sparse Core Ops, SparseCore 0:
  14.2 36.8 reduce-scatter.2
  52.7 23.5 all-gather.10
  78.6 42.9 all-gather.16
  123.1 38.6 all-gather.14
  193.3 33.0 reduce-scatter.4
  227.9 23.5 all-gather.12
  253.8 42.9 all-gather.20
  298.4 38.6 all-gather.18
